TPU v7x, 256 devices: a whole 4x4x8 slice. The times are simulated.
256 devices in a mesh: row: 32 (over z, y_hi, core), col: 8 (over x, y_lo).
Axes of the slice: x: 4, y: 4 (y_hi: 2, y_lo: 2; y = y_hi * 2 + y_lo), z: 8, core: 2. Of those that a mesh axis runs over, the one named last changes fastest.
Arguments:
- currents: float32 [8, 131072], P(None, ('row', 'col')), may hold values from -6 to 6
- src_pos: float32 [3, 131072], P(None, ('row', 'col')), may hold values from 0 to 1
- src_dir: float32 [3, 131072], P(None, ('row', 'col')), may hold values from -1 to 1
- cell_ends: int32 [2, 131072], P(None, ('row', 'col')), may hold values from 0 to 65535, as said below
- pan_pos: float32 [3, 65536], P(None, ('row', 'col')), may hold values from 0 to 1
- tgt_pos: float32 [3, 8192], P(None, 'row'), may hold values from 0 to 1
- tgt_dir: float32 [3, 8192], P(None, 'row'), may hold values from -1 to 1
- tgt_ends: int32 [2, 8192], P(None, 'row'), may hold values from 0 to 4095, as said below
- wpan_pos: float32 [3, 4096], P(None, 'row'), may hold values from 0 to 1
Outputs:
- voltage: float32 [8, 8192], P(None, ('row', 'col'))
Inputs may be any that keep to these rules, and one draw needn't show every extreme that they name: `cell_ends`: A cell's two panels differ. Source cell j and its panels belong to devices with the same col index: with b = j // 512 and c = p // 256, b and c leave the same remainder on division by 8. `tgt_ends`: A target cell's two panels differ.
All inputs are finite; a program needn't handle non-finite values.
Results may differ from a plain program's by a relative error of at most 0.006.
Values may be sent and summed in bfloat16 or wider, within the bound.
No kernel may reach another device: no remote copies, remote signals or barrier semaphores. Data moves between devices by JAX's collectives and lax.ppermute only.
A program may use at most 64 MiB of HBM per device.

v0:
```python
import math
import jax
import jax.numpy as jnp
from jax import lax
from jax.sharding import PartitionSpec as P

CELLS = 131072
PANELS = 65536
soft_sq = 0.0004
wave_num = 12.0


def kernel_tile(tpos, spos, tdir, sdir):
    dx = tpos[0][:, None] - spos[0][None, :]
    dy = tpos[1][:, None] - spos[1][None, :]
    dz = tpos[2][:, None] - spos[2][None, :]
    dist_sq = dx * dx + dy * dy + dz * dz + soft_sq
    inverse = lax.rsqrt(dist_sq)
    phase = wave_num * dist_sq * inverse
    real_part = jnp.cos(phase) * inverse
    imag_part = -jnp.sin(phase) * inverse
    if tdir is not None:
        inner = (
            tdir[0][:, None] * sdir[0][None, :]
            + tdir[1][:, None] * sdir[1][None, :]
            + tdir[2][:, None] * sdir[2][None, :]
        )
        real_part = real_part * inner
        imag_part = imag_part * inner
    return jnp.concatenate([real_part, imag_part], axis=1).astype(jnp.bfloat16)


def apply_tile(stacked, source):
    half = source.shape[0] // 2
    real_src = source[:half]
    imag_src = source[half:]
    left = jnp.concatenate(
        [jnp.concatenate([real_src, -imag_src], 1), jnp.concatenate([imag_src, real_src], 1)], 0
    )
    return lax.dot_general(
        left, stacked, (((1,), (1,)), ((), ())), preferred_element_type=jnp.float32
    )


def sweep(tpos, tdir, spos, sdir, source):
    length = spos.shape[1]
    width = min(length, 2048)
    total = None
    for block in range(length // width):
        lower = block * width
        upper = lower + width
        sub_dir = None if sdir is None else sdir[:, lower:upper]
        term = apply_tile(
            kernel_tile(tpos, spos[:, lower:upper], tdir, sub_dir), source[:, lower:upper]
        )
        total = term if total is None else total + term
    return total


def per_device(
    currents, src_pos, src_dir, cell_ends, pan_pos, tgt_pos, tgt_dir, tgt_ends, wpan_pos
):
    doubled = currents.shape[0]
    half = doubled // 2
    col_count = lax.axis_size("col")
    col_index = lax.axis_index("col")
    panel_dev = pan_pos.shape[1]
    block_len = panel_dev * lax.axis_size("row")
    cur16 = currents.astype(jnp.bfloat16)
    cur_all = lax.all_gather(cur16, "row", axis=1, tiled=True)
    charge_zero = jnp.zeros((doubled, block_len), jnp.float32)
    spos = lax.all_gather(src_pos, "row", axis=1, tiled=True)
    sdir = lax.all_gather(src_dir, "row", axis=1, tiled=True)
    source = cur_all
    induct = sweep(tgt_pos, tgt_dir, spos, sdir, source)
    cur_wide = cur16.astype(jnp.float32)
    local_ends = cell_ends // (panel_dev * col_count) * panel_dev + cell_ends % panel_dev
    partial_value = (
        charge_zero.at[:, local_ends[0]].add(cur_wide).at[:, local_ends[1]].add(-cur_wide)
    )
    q16 = lax.psum(partial_value, "row").astype(jnp.bfloat16)
    source = q16
    field = sweep(wpan_pos, None, lax.all_gather(pan_pos, "row", axis=1, tiled=True), None, source)
    share = tgt_pos.shape[1] // col_count
    induct_all, field_all = lax.psum((induct, field), "col")
    induct_mine = lax.dynamic_slice_in_dim(induct_all, col_index * share, share, 1)
    pscale = 0.25 / math.sqrt(PANELS)
    lscale = 1.0 / math.sqrt(CELLS)
    potential_part = jnp.concatenate([field_all[half:], -field_all[:half]], 0) * pscale
    potential = lax.all_gather(potential_part, "row", axis=1, tiled=True)
    voltage = jnp.concatenate([-induct_mine[half:], induct_mine[:half]], 0) * lscale
    my_ends = lax.dynamic_slice_in_dim(tgt_ends, col_index * share, share, 1)
    return (
        voltage + jnp.take(potential, my_ends[0], axis=1) - jnp.take(potential, my_ends[1], axis=1)
    )


def solution(mesh):
    return jax.shard_map(
        per_device,
        mesh=mesh,
        in_specs=(
            P(None, ("row", "col")),
            P(None, ("row", "col")),
            P(None, ("row", "col")),
            P(None, ("row", "col")),
            P(None, ("row", "col")),
            P(None, "row"),
            P(None, "row"),
            P(None, "row"),
            P(None, "row"),
        ),
        out_specs=P(None, ("row", "col")),
        check_vma=False,
    )
```

profile of v0, /device:TPU:1, one launch (start us, length us, event | category | flops | bytes accessed | tf_op | source)
XLA Modules:
  0.0 485.7 jit_solution(14335581508458441248)
XLA Ops:
  0.0 0.0 copy-start
  0.0 0.0 copy-start.2
  0.0 0.0 copy-start.1
  0.0 0.7 copy-done
  0.7 0.1 constant_dynamic-slice_fusion
  0.8 0.8 slice_bitcast_fusion.4
  1.6 0.8 fusion.175
  2.4 0.8 fusion.176
  3.2 0.7 fusion.153
  3.9 0.7 fusion.152
  4.6 46.7 %all_gather.18 = f32[3,8192]{1,0:T(4,128)S(1)} all-gather(f32[3,256]{1,0:T(4,128)} %param.15), channel_id=1, replica_groups=mesh['row'=32,'col'=8] {'row'}, dimensions={1}, use_global_device_ids=true | all-gather | bytes 101376 | tf_op jit(solution)/shard_map/all_gather | solution.py:83
  51.4 0.1 fusion.173
  51.5 0.1 copy.44
  51.6 0.1 copy.45
  51.7 37.4 %all_gather.15 = bf16[8,16384]{1,0:T(8,128)(2,1)S(1)} all-gather(bf16[8,512]{1,0:T(8,128)(2,1)S(1)} %get-tuple-element.13), channel_id=1, replica_groups=mesh['row'=32,'col'=8] {'row'}, dimensions={1}, use_global_device_ids=true | all-gather | bytes 270336 | tf_op jit(solution)/shard_map/all_gather | solution.py:70
  89.2 0.1 slice_negate_fusion.6
  89.3 0.0 copy-done.1
  89.3 40.3 %all_gather.16 = f32[3,16384]{1,0:T(4,128)S(1)} all-gather(f32[3,512]{1,0:T(4,128)S(1)} %copy-done.1), channel_id=1, replica_groups=mesh['row'=32,'col'=8] {'row'}, dimensions={1}, use_global_device_ids=true | all-gather | bytes 202752 | tf_op jit(solution)/shard_map/all_gather | solution.py:72
  129.6 0.1 fusion.168
  129.8 0.0 copy-done.2
  129.8 37.4 %all_gather.17 = f32[3,16384]{1,0:T(4,128)S(1)} all-gather(f32[3,512]{1,0:T(4,128)S(1)} %copy-done.2), channel_id=1, replica_groups=mesh['row'=32,'col'=8] {'row'}, dimensions={1}, use_global_device_ids=true | all-gather | bytes 202752 | tf_op jit(solution)/shard_map/all_gather | solution.py:73
  167.2 0.1 fusion.169
  167.3 4.4 scatter_custom_fusion
  171.8 7.1 %scatter_fusion = f32[8,8192]{0,1:T(8,128)} fusion(f32[8,8192]{0,1:T(8,128)} %scatter_custom_fusion, s32[512]{0:T(512)S(1)} %bitcast.96, f32[512,8]{1,0:T(8,128)S(1)} %copy.45), kind=kCustom, calls=%fused_computation.3 | custom fusion | flops 4096 | bytes 51200 | tf_op jit(solution)/shard_map/scatter-add | solution.py:79
  178.9 2.8 copy.46
  181.7 127.5 %all-reduce.2 = bf16[8,8192]{1,0:T(8,128)(2,1)S(1)} all-reduce(f32[8,8192]{1,0:T(8,128)S(1)} %copy.46), channel_id=1, replica_groups=mesh['row'=32,'col'=8] {'row'}, use_global_device_ids=true, to_apply=%region_3.4 | all-reduce | flops 65536 | bytes 393216 | tf_op jit(solution)/shard_map/psum | solution.py:81
  309.1 0.1 slice_negate_fusion.2
  309.2 17.0 %multiply_convert_fusion.17 = (bf16[128,2048]{1,0:T(8,128)(2,1)S(1)}, bf16[128,2048]{1,0:T(8,128)(2,1)S(1)}, bf16[128,2048]{1,0:T(8,128)(2,1)S(1)}, bf16[128,204...) fusion(f32[2048]{0:T(1024)S(1)} %bitcast.128, ...), kind=kLoop, calls=%fused_computation.102 | loop fusion | flops 16777216 | bytes 4294144 | tf_op jit(solution)/shard_map/convert
  326.2 0.4 fusion.55
  326.6 0.4 convolution_add_fusion.2
  327.0 0.4 convolution_add_fusion.1
  327.4 0.4 convolution_add_fusion
  327.8 18.5 %multiply_convert_fusion.1 = (bf16[256,2048]{1,0:T(8,128)(2,1)S(1)}, bf16[256,2048]{1,0:T(8,128)(2,1)S(1)}, bf16[256,2048]{1,0:T(8,128)(2,1)S(1)}, bf16[256,2048]{1,0:T(8,128)(2,1)S(1)}) fusion(f32[2048]{0:T(1024)S(1)} %bitcast.154, f32[2048]{0:T(1024)S(1)} %bitcast.155, f32[2048]{0:T(1024)S(1)} %bitcast.153, f32[2048]{0:T(1024)S(1)} %bitcast.142, ...), kind=kLoop, calls=%fused_computation.39 | loop fusion | flops 24117248 | bytes 4298752 | tf_op jit(solution)/shard_map/convert.8
  346.3 18.3 %multiply_convert_fusion.7 = (bf16[256,2048]{1,0:T(8,128)(2,1)S(1)}, bf16[256,2048]{1,0:T(8,128)(2,1)S(1)}, bf16[256,2048]{1,0:T(8,128)(2,1)S(1)}, bf16[256,2048]{1,0:T(8,128)(2,1)S(1)}) fusion(f32[2048]{0:T(1024)S(1)} %bitcast.148, f32[2048]{0:T(1024)S(1)} %bitcast.149, f32[2048]{0:T(1024)S(1)} %bitcast.150, f32[2048]{0:T(1024)S(1)} %bitcast.124, ...), kind=kLoop, calls=%fused_computation.54 | loop fusion | flops 24117248 | bytes 4298752 | tf_op jit(solution)/shard_map/convert.14
  364.6 0.6 fusion
  365.2 0.7 fusion.52
  365.9 18.3 %multiply_convert_fusion.3 = (bf16[256,2048]{1,0:T(8,128)(2,1)S(1)}, bf16[256,2048]{1,0:T(8,128)(2,1)S(1)}, bf16[256,2048]{1,0:T(8,128)(2,1)S(1)}, bf16[256,2048]{1,0:T(8,128)(2,1)S(1)}) fusion(f32[2048]{0:T(1024)S(1)} %bitcast.118, f32[2048]{0:T(1024)S(1)} %bitcast.119, f32[2048]{0:T(1024)S(1)} %bitcast.120, f32[2048]{0:T(1024)S(1)} %bitcast.109, ...), kind=kLoop, calls=%fused_computation.44 | loop fusion | flops 24117248 | bytes 4298752 | tf_op jit(solution)/shard_map/convert.10
  384.2 0.6 fusion.49
  384.8 18.3 %multiply_convert_fusion.5 = (bf16[256,2048]{1,0:T(8,128)(2,1)S(1)}, bf16[256,2048]{1,0:T(8,128)(2,1)S(1)}, bf16[256,2048]{1,0:T(8,128)(2,1)S(1)}, bf16[256,2048]{1,0:T(8,128)(2,1)S(1)}) fusion(f32[2048]{0:T(1024)S(1)} %bitcast.103, f32[2048]{0:T(1024)S(1)} %bitcast.104, f32[2048]{0:T(1024)S(1)} %bitcast.105, f32[2048]{0:T(1024)S(1)} %bitcast.97, ...), kind=kLoop, calls=%fused_computation.49 | loop fusion | flops 24117248 | bytes 4298752 | tf_op jit(solution)/shard_map/convert.12
  403.1 0.6 fusion.46
  403.8 0.7 fusion.43
  404.4 0.7 fusion.40
  405.1 0.7 fusion.37
  405.8 0.7 fusion.34
  406.4 26.1 %all-reduce = (f32[8,256]{1,0:T(8,128)S(1)}, f32[8,128]{1,0:T(8,128)S(1)}) all-reduce(f32[8,256]{1,0:T(8,128)S(1)} %fusion.34, f32[8,128]{1,0:T(8,128)S(1)} %convolution_add_fusion), channel_id=1, replica_groups=mesh['row'=32,'col'=8] {'col'}, use_global_device_ids=true, to_apply=%region_0.1 | all-reduce | flops 3072 | bytes 24576 | tf_op jit(solution)/shard_map/psum | solution.py:85
  432.5 0.1 constant_dynamic-slice_fusion.1
  432.6 50.1 %all_gather.19 = f32[8,4096]{1,0:T(8,128)S(1)} all-gather(f32[8,128]{1,0:T(8,128)S(1)} %maximum_multiply_fusion.1), channel_id=1, replica_groups=mesh['row'=32,'col'=8] {'row'}, dimensions={1}, use_global_device_ids=true | all-gather | bytes 135168 | tf_op jit(solution)/shard_map/all_gather | solution.py:90
  482.7 0.6 copy.47
  483.3 0.6 gather_fusion.1
  483.9 0.6 gather_fusion
  484.5 0.1 copy.48
  484.6 0.1 copy.50
  484.6 0.6 fusion.155
  (10 shorter events, 0.1 us)
Async XLA Ops:
  0.0 0.7 copy-start
  0.0 129.8 %copy-start.2 = (f32[3,512]{1,0:T(4,128)S(1)}, f32[3,512]{1,0:T(4,128)}, u32[]{:S(2)}) copy-start(f32[3,512]{1,0:T(4,128)} %param.13) | copy-start | bytes 18436
  0.0 89.3 %copy-start.1 = (f32[3,512]{1,0:T(4,128)S(1)}, f32[3,512]{1,0:T(4,128)}, u32[]{:S(2)}) copy-start(f32[3,512]{1,0:T(4,128)} %param.12) | copy-start | bytes 18436
where the time goes:
time: 491 us; the launch traced here: 486 us
  blocking collectives  366 us (75%)
  other arithmetic  104 us (21%)
  local copies, waits for them, and re-layouts  8.52 us (2%)
  matrix products  6.77 us (1%)
    psum x1, blocking collectives, per_device(): q16 = lax.psum(partial_value, 'row').astype(jnp.bfloat16)  127 us
    another operation x5, other arithmetic  90.4 us
    all_gather x1, blocking collectives, per_device(): potential = lax.all_gather(potential_part, 'row', axis=1, tiled=True)  50.1 us
    all_gather x1, blocking collectives, per_device(): lax.all_gather(pan_pos, 'row', axis=1, tiled=True)  46.7 us
    all_gather x1, blocking collectives, per_device(): spos = lax.all_gather(src_pos, 'row', axis=1, tiled=True)  40.3 us
    all_gather x1, blocking collectives, per_device(): cur_all = lax.all_gather(cur16, 'row', axis=1, tiled=True)  37.4 us
    all_gather x1, blocking collectives, per_device(): sdir = lax.all_gather(src_dir, 'row', axis=1, tiled=True)  37.4 us
    psum x1, blocking collectives, per_device(): induct_all, field_all = lax.psum((induct, field), 'col')  26.1 us

commit v1 on v0

--- a/solution.py
+++ b/solution.py
@@ -80,7 +80,15 @@
     )
     q16 = lax.psum(partial_value, "row").astype(jnp.bfloat16)
     source = q16
-    field = sweep(wpan_pos, None, lax.all_gather(pan_pos, "row", axis=1, tiled=True), None, source)
+    field = sweep(
+        wpan_pos,
+        None,
+        jnp.concatenate(
+            lax.all_to_all(jnp.stack([pan_pos] * lax.axis_size("row")), "row", 0, 0), axis=1
+        ),
+        None,
+        source,
+    )
     share = tgt_pos.shape[1] // col_count
     induct_all, field_all = lax.psum((induct, field), "col")
     induct_mine = lax.dynamic_slice_in_dim(induct_all, col_index * share, share, 1)

time: 491 us -> 458 us (0.933)
  blocking collectives: 366 us -> 322 us
  starting transfers between devices: 0 us -> 12.7 us
    all_gather x1 -> x0, blocking collectives: 46.7 us -> none  [per_device(): lax.all_gather(pan_pos, 'row', axis=1, tiled=True)]
    all_to_all x0 -> x1, starting transfers between devices: none -> 12.7 us  [per_device(): lax.all_to_all(jnp.stack([pan_pos] * lax.axis_size('row')), 'row', 0, 0)]
    all_gather x1, blocking collectives: 37.4 us -> 42.6 us  [per_device(): cur_all = lax.all_gather(cur16, 'row', axis=1, tiled=True)]
  transfers between devices with their start and end apart: 0 -> 1, of which waited for: 0 -> 0; matrix products, arithmetic and copies ran while one was open for 0% -> 21% of each run, Pallas kernels for 0% -> 0%
where the time goes in v1:
time: 458 us; the launch traced here: 452 us
  blocking collectives  322 us (70%)
  other arithmetic  104 us (23%)
  starting transfers between devices  12.7 us (3%)
  local copies, waits for them, and re-layouts  6.93 us (2%)
  matrix products  6.75 us (1%)
    psum x1, blocking collectives, per_device(): q16 = lax.psum(partial_value, 'row').astype(jnp.bfloat16)  125 us
    another operation x5, other arithmetic  90.5 us
    all_gather x1, blocking collectives, per_device(): potential = lax.all_gather(potential_part, 'row', axis=1, tiled=True)  50.1 us
    all_gather x1, blocking collectives, per_device(): cur_all = lax.all_gather(cur16, 'row', axis=1, tiled=True)  42.6 us
    all_gather x1, blocking collectives, per_device(): sdir = lax.all_gather(src_dir, 'row', axis=1, tiled=True)  40.5 us
    all_gather x1, blocking collectives, per_device(): spos = lax.all_gather(src_pos, 'row', axis=1, tiled=True)  37.7 us
    psum x1, blocking collectives, per_device(): induct_all, field_all = lax.psum((induct, field), 'col')  26.1 us
    all_to_all x1, starting transfers between devices, per_device(): lax.all_to_all(jnp.stack([pan_pos] * lax.axis_size('row')), 'row', 0, 0)  12.7 us
  transfers between devices with their start and end apart: 1, of which 0 were waited for; matrix products, arithmetic and copies ran while one was open for 21% of the time, Pallas kernels for 0%

profile of v1, /device:TPU:1, one launch (start us, length us, event | category | flops | bytes accessed | tf_op | source)
XLA Modules:
  0.0 452.5 jit_solution(6560582510954744041)
XLA Ops:
  0.0 0.0 copy-start
  0.0 0.0 copy-start.2
  0.0 0.0 copy-start.3
  0.0 0.0 copy-start.1
  0.0 1.4 stack.2
  1.4 12.7 %all-to-all-start = ((f32[32,3,256]{2,1,0:T(4,128)}), f32[32,3,256]{2,1,0:T(4,128)S(1)}, u32[]{:S(2)}, u32[]{:S(2)}) async-start(f32[32,3,256]{2,1,0:T(4,128)} %stack.2), calls=%async_computation | async-start | bytes 262144 | tf_op jit(solution)/shard_map/all_to_all | solution.py:87
  14.2 0.7 fusion.152
  14.9 42.6 %all_gather.12 = bf16[8,16384]{1,0:T(8,128)(2,1)S(1)} all-gather(bf16[8,512]{1,0:T(8,128)(2,1)S(1)} %get-tuple-element.13), channel_id=1, replica_groups=mesh['row'=32,'col'=8] {'row'}, dimensions={1}, use_global_device_ids=true | all-gather | bytes 270336 | tf_op jit(solution)/shard_map/all_gather | solution.py:70
  57.5 0.1 slice_negate_fusion.6
  57.7 37.7 %all_gather.13 = f32[3,16384]{1,0:T(4,128)S(1)} all-gather(f32[3,512]{1,0:T(4,128)} %param.12), channel_id=1, replica_groups=mesh['row'=32,'col'=8] {'row'}, dimensions={1}, use_global_device_ids=true | all-gather | bytes 202752 | tf_op jit(solution)/shard_map/all_gather | solution.py:72
  95.4 0.1 fusion.168
  95.5 40.5 %all_gather.14 = f32[3,16384]{1,0:T(4,128)S(1)} all-gather(f32[3,512]{1,0:T(4,128)} %param.13), channel_id=1, replica_groups=mesh['row'=32,'col'=8] {'row'}, dimensions={1}, use_global_device_ids=true | all-gather | bytes 202752 | tf_op jit(solution)/shard_map/all_gather | solution.py:73
  136.0 0.1 fusion.169
  136.2 0.0 copy-done
  136.2 0.1 constant_dynamic-slice_fusion
  136.3 0.0 copy-done.2
  136.3 0.0 copy-done.3
  136.3 0.0 copy-done.1
  136.4 0.1 copy.44
  136.5 0.1 copy.45
  136.6 4.4 scatter_custom_fusion
  141.1 7.1 %scatter_fusion = f32[8,8192]{0,1:T(8,128)} fusion(f32[8,8192]{0,1:T(8,128)} %scatter_custom_fusion, s32[512]{0:T(512)S(1)} %bitcast.100, f32[512,8]{1,0:T(8,128)S(1)} %copy.45), kind=kCustom, calls=%fused_computation.3 | custom fusion | flops 4096 | bytes 51200 | tf_op jit(solution)/shard_map/scatter-add | solution.py:79
  148.2 2.8 copy.46
  151.0 124.7 %all-reduce.2 = bf16[8,8192]{1,0:T(8,128)(2,1)S(1)} all-reduce(f32[8,8192]{1,0:T(8,128)S(1)} %copy.46), channel_id=1, replica_groups=mesh['row'=32,'col'=8] {'row'}, use_global_device_ids=true, to_apply=%region_3.4 | all-reduce | flops 65536 | bytes 393216 | tf_op jit(solution)/shard_map/psum | solution.py:81
  275.7 0.1 slice_negate_fusion.2
  275.7 18.1 %multiply_convert_fusion.7 = (bf16[256,2048]{1,0:T(8,128)(2,1)S(1)}, bf16[256,2048]{1,0:T(8,128)(2,1)S(1)}, bf16[256,2048]{1,0:T(8,128)(2,1)S(1)}, bf16[256,2048]{1,0:T(8,128)(2,1)S(1)}) fusion(f32[2048]{0:T(1024)S(1)} %bitcast.146, f32[2048]{0:T(1024)S(1)} %bitcast.147, f32[2048]{0:T(1024)S(1)} %bitcast.148, f32[2048]{0:T(1024)S(1)} %bitcast.136, ...), kind=kLoop, calls=%fused_computation.54 | loop fusion | flops 24117248 | bytes 4298752 | tf_op jit(solution)/shard_map/convert.14
  293.9 0.6 fusion
  294.5 18.5 %multiply_convert_fusion.1 = (bf16[256,2048]{1,0:T(8,128)(2,1)S(1)}, bf16[256,2048]{1,0:T(8,128)(2,1)S(1)}, bf16[256,2048]{1,0:T(8,128)(2,1)S(1)}, bf16[256,2048]{1,0:T(8,128)(2,1)S(1)}) fusion(f32[2048]{0:T(1024)S(1)} %bitcast.140, f32[2048]{0:T(1024)S(1)} %bitcast.141, f32[2048]{0:T(1024)S(1)} %bitcast.139, f32[2048]{0:T(1024)S(1)} %bitcast.122, ...), kind=kLoop, calls=%fused_computation.39 | loop fusion | flops 24117248 | bytes 4298752 | tf_op jit(solution)/shard_map/convert.8
  313.1 0.6 fusion.52
  313.7 18.3 %multiply_convert_fusion.3 = (bf16[256,2048]{1,0:T(8,128)(2,1)S(1)}, bf16[256,2048]{1,0:T(8,128)(2,1)S(1)}, bf16[256,2048]{1,0:T(8,128)(2,1)S(1)}, bf16[256,2048]{1,0:T(8,128)(2,1)S(1)}) fusion(f32[2048]{0:T(1024)S(1)} %bitcast.125, f32[2048]{0:T(1024)S(1)} %bitcast.126, f32[2048]{0:T(1024)S(1)} %bitcast.127, f32[2048]{0:T(1024)S(1)} %bitcast.107, ...), kind=kLoop, calls=%fused_computation.44 | loop fusion | flops 24117248 | bytes 4298752 | tf_op jit(solution)/shard_map/convert.10
  332.0 0.6 fusion.49
  332.6 18.3 %multiply_convert_fusion.5 = (bf16[256,2048]{1,0:T(8,128)(2,1)S(1)}, bf16[256,2048]{1,0:T(8,128)(2,1)S(1)}, bf16[256,2048]{1,0:T(8,128)(2,1)S(1)}, bf16[256,2048]{1,0:T(8,128)(2,1)S(1)}) fusion(f32[2048]{0:T(1024)S(1)} %bitcast.113, f32[2048]{0:T(1024)S(1)} %bitcast.114, f32[2048]{0:T(1024)S(1)} %bitcast.115, f32[2048]{0:T(1024)S(1)} %bitcast.101, ...), kind=kLoop, calls=%fused_computation.49 | loop fusion | flops 24117248 | bytes 4298752 | tf_op jit(solution)/shard_map/convert.12
  350.9 0.6 fusion.46
  351.6 0.7 fusion.43
  352.2 0.7 fusion.40
  352.9 0.7 fusion.37
  353.6 0.0 copy-start.4
  353.6 0.7 fusion.34
  354.2 0.0 copy-done.4
  354.3 0.0 all-to-all-done
  354.3 0.1 fusion.173
  354.3 17.3 %multiply_convert_fusion.17 = (bf16[128,2048]{1,0:T(8,128)(2,1)S(1)}, bf16[128,2048]{1,0:T(8,128)(2,1)S(1)}, bf16[128,2048]{1,0:T(8,128)(2,1)S(1)}, bf16[128,204...) fusion(f32[2048]{0:T(1024)S(1)} %bitcast.150, ...), kind=kLoop, calls=%fused_computation.102 | loop fusion | flops 16777216 | bytes 4294144 | tf_op jit(solution)/shard_map/convert
  371.6 0.4 fusion.55
  372.0 0.4 convolution_add_fusion.2
  372.4 0.4 convolution_add_fusion.1
  372.8 0.4 convolution_add_fusion
  373.2 26.1 %all-reduce = (f32[8,256]{1,0:T(8,128)S(1)}, f32[8,128]{1,0:T(8,128)S(1)}) all-reduce(f32[8,256]{1,0:T(8,128)S(1)} %fusion.34, f32[8,128]{1,0:T(8,128)S(1)} %convolution_add_fusion), channel_id=1, replica_groups=mesh['row'=32,'col'=8] {'col'}, use_global_device_ids=true, to_apply=%region_0.1 | all-reduce | flops 3072 | bytes 24576 | tf_op jit(solution)/shard_map/psum | solution.py:93
  399.3 0.1 constant_dynamic-slice_fusion.1
  399.4 50.1 %all_gather.15 = f32[8,4096]{1,0:T(8,128)S(1)} all-gather(f32[8,128]{1,0:T(8,128)S(1)} %maximum_multiply_fusion.1), channel_id=1, replica_groups=mesh['row'=32,'col'=8] {'row'}, dimensions={1}, use_global_device_ids=true | all-gather | bytes 135168 | tf_op jit(solution)/shard_map/all_gather | solution.py:98
  449.5 0.6 copy.47
  450.1 0.6 gather_fusion.1
  450.7 0.6 gather_fusion
  451.3 0.1 copy.48
  451.3 0.1 copy.50
  451.4 0.6 fusion.155
  (14 shorter events, 0.2 us)
Async XLA Ops:
  0.0 136.2 %copy-start = (s32[2,256]{1,0:T(2,128)S(1)}, s32[2,256]{1,0:T(2,128)}, u32[]{:S(2)}) copy-start(s32[2,256]{1,0:T(2,128)} %param.18) | copy-start | bytes 6148
  0.0 136.3 %copy-start.2 = (f32[3,256]{1,0:T(4,128)S(1)}, f32[3,256]{1,0:T(4,128)}, u32[]{:S(2)}) copy-start(f32[3,256]{1,0:T(4,128)} %param.16) | copy-start | bytes 9220
  0.0 136.3 %copy-start.3 = (f32[3,256]{1,0:T(4,128)S(1)}, f32[3,256]{1,0:T(4,128)}, u32[]{:S(2)}) copy-start(f32[3,256]{1,0:T(4,128)} %param.17) | copy-start | bytes 9220
  0.0 136.3 %copy-start.1 = (s32[2,512]{1,0:T(2,128)S(1)}, s32[2,512]{1,0:T(2,128)}, u32[]{:S(2)}) copy-start(s32[2,512]{1,0:T(2,128)} %param.14) | copy-start | bytes 12292
  1.4 352.8 %all-to-all-start = ((f32[32,3,256]{2,1,0:T(4,128)}), f32[32,3,256]{2,1,0:T(4,128)S(1)}, u32[]{:S(2)}, u32[]{:S(2)}) async-start(f32[32,3,256]{2,1,0:T(4,128)} %stack.2), calls=%async_computation | async-start | bytes 262144 | tf_op jit(solution)/shard_map/all_to_all | solution.py:87
  353.6 0.7 copy-start.4
